TPU v7x, 32 devices: a whole 2x2x4 slice. The times are simulated.
32 devices in a mesh: ev: 16 (over z, y, core), st: 2 (over x).
Axes of the slice: x: 2, y: 2, z: 4, core: 2. Of those that a mesh axis runs over, the one named last changes fastest.
Arguments:
- strain: bfloat16 [2, 6, 256, 4096], P(None, None, 'ev'), may hold values from -0.068359375 to 0.068359375
- green: bfloat16 [2, 3, 256, 6, 4096], P(None, None, 'st', None, 'ev'), may hold values from -6 to 6
- weights: bfloat16 [2, 3, 256, 256], P(None, None, 'ev', 'st'), may hold values from -0.15625 to 0.15625
- mask: int32 [256, 256], P('ev', 'st'), may hold values 0 or 1
Outputs:
- kernels: float32 [2, 4096], P(None, ('ev', 'st'))
All inputs are finite; a program needn't handle non-finite values. No bound on the sum of `mask` on one device may be relied on, other than what follows from the above.
Results may differ from a plain program's by a relative error of at most 0.0003.
Values may be sent and summed in bfloat16 or wider, within the bound.
No kernel may reach another device: no remote copies, remote signals or barrier semaphores. Data moves between devices by JAX's collectives and lax.ppermute only.
A program may use at most 128 MiB of HBM per device.

v0:
```python
import jax
import jax.numpy as jnp
from jax import lax
from jax.sharding import PartitionSpec as P


def local(strain, green, weights, mask):
    masked = weights * mask.astype(jnp.bfloat16)[None, None]
    cells_dev = green.shape[4]
    station_count = green.shape[2]
    event_rows = strain.shape[2]
    ev_count = lax.axis_size("ev")
    st_count = lax.axis_size("st")
    sub_cells = cells_dev // st_count
    shaped = strain.reshape(2, 6, event_rows, ev_count, st_count, sub_cells)
    selected = lax.dynamic_index_in_dim(shaped, lax.axis_index("st"), 4, keepdims=False)
    selected = selected.reshape(2, 6, event_rows, ev_count * sub_cells)
    narrow = lax.all_to_all(selected, "ev", split_axis=3, concat_axis=2, tiled=True)
    strain_all = lax.all_gather(narrow, "st", axis=3, tiled=True)
    green_flat = green.reshape(2, 3, station_count, 6 * cells_dev)
    voigt = jnp.array([1.0, 1.0, 1.0, 2.0, 2.0, 2.0], jnp.float32)
    weight_rows = lax.all_gather(masked, "ev", axis=2, tiled=True)
    row_count = weight_rows.shape[2]
    products = jnp.einsum(
        "rfps,qfsn->rqpn", weight_rows, green_flat, preferred_element_type=jnp.float32
    )
    held_real = (products[0, 0] - products[1, 1]).reshape(row_count, 6, cells_dev)
    held_imag = (products[0, 1] + products[1, 0]).reshape(row_count, 6, cells_dev)
    strain_rows = strain_all.astype(jnp.float32)
    strain_real = jnp.swapaxes(strain_rows[0], 0, 1)
    strain_imag = jnp.swapaxes(strain_rows[1], 0, 1)
    trace_term = jnp.sum(
        strain_real[:, :3].sum(1) * held_real[:, :3].sum(1)
        - strain_imag[:, :3].sum(1) * held_imag[:, :3].sum(1),
        axis=0,
    )
    shear_term = jnp.sum(
        (strain_real * held_real - strain_imag * held_imag) * voigt[None, :, None], axis=(0, 1)
    )
    partial_value = jnp.stack([trace_term, shear_term])
    return lax.psum_scatter(partial_value, "st", scatter_dimension=1, tiled=True)


def solution(mesh):
    placed = (
        P(None, None, "ev", None),
        P(None, None, "st", None, "ev"),
        P(None, None, "ev", "st"),
        P("ev", "st"),
    )
    return jax.shard_map(
        local, mesh=mesh, in_specs=placed, out_specs=P(None, ("ev", "st")), check_vma=False
    )
```

profile of v0, /device:TPU:0, one launch (start us, length us, event | category | flops | bytes accessed | tf_op | source)
XLA Modules:
  0.0 143.1 jit_solution(11234989107015068082)
XLA Ops:
  6.5 2.8 %reshape.20 = bf16[2,6,16,16,2,128]{5,4,3,2,1,0:T(2,128)(2,1)S(1)} reshape(bf16[2,6,16,4096]{3,2,1,0:T(8,128)(2,1)} %param.5) | data formatting | bytes 3145728 | tf_op jit(solution)/shard_map/reshape | solution.py:15
  9.4 1.9 %constant_dynamic-slice_fusion = bf16[2,6,16,16,1,128]{5,4,3,2,1,0:T(2,128)(2,1)S(1)} fusion(bf16[2,6,16,16,2,128]{5,4,3,2,1,0:T(2,128)(2,1)S(1)} %reshape.20, s32[]{:T(128)S(6)} %select_n.4), kind=kLoop, calls=%fused_computation.14 | loop fusion | bytes 1572868 | tf_op jit(solution)/shard_map/jit(dynamic_index_in_dim)/dynamic_slice | solution.py:16
  11.3 11.5 %copy.44 = bf16[2,6,16,16,1,128]{2,0,1,5,3,4:T(2,128)(2,1)} copy(bf16[2,6,16,16,1,128]{5,4,3,2,1,0:T(2,128)(2,1)S(1)} %constant_dynamic-slice_fusion) | data formatting | bytes 1572864 | tf_op jit(solution)/shard_map/reshape | solution.py:17
  22.8 18.4 %reshape.28 = bf16[16,2,12288]{2,1,0:T(2,128)(2,1)} reshape(bf16[2048,6,2,16]{3,2,1,0:T(2,128)(2,1)} %bitcast.43) | data formatting | bytes 1572864
  41.2 7.5 %all-to-all-start = ((bf16[16,2,12288]{2,1,0:T(2,128)(2,1)}), bf16[16,2,12288]{2,1,0:T(2,128)(2,1)S(1)}, u32[]{:S(2)}, u32[]{:S(2)}) async-start(bf16[16,2,12288]{2,1,0:T(2,128)(2,1)} %reshape.28), calls=%async_computation | async-start | bytes 1572864 | tf_op jit(solution)/shard_map/all_to_all | solution.py:18
  48.7 0.0 all-gather.2.cloned.1.call-start
  48.8 3.1 %copy.33 = bf16[2,3,128,6,256]{2,4,3,1,0:T(8,128)(2,1)S(1)} copy(bf16[2,3,128,6,256]{4,2,3,1,0:T(8,128)(2,1)} %param.6) | data formatting | bytes 4718592 | tf_op args[1]
  51.9 15.5 %all-to-all-done = bf16[16,2,12288]{2,1,0:T(2,128)(2,1)S(1)} async-done(((bf16[16,2,12288]{2,1,0:T(2,128)(2,1)}), bf16[16,2,12288]{2,1,0:T(2,128)(2,1)S(1)}, u32[]{:S(2)}, u32[]{:S(2)}) %all-to-all-start) | async-done | bytes 786464 | tf_op jit(solution)/shard_map/all_to_all | solution.py:18
  67.4 5.6 %reshape.29 = bf16[2048,6,2,16]{3,2,1,0:T(2,128)(2,1)} reshape(bf16[16,2,12288]{2,1,0:T(2,128)(2,1)S(1)} %all-to-all-done) | data formatting | bytes 1572864
  73.0 14.8 %copy.46 = bf16[2,6,16,16,128]{4,2,3,1,0:T(8,128)(2,1)} copy(bf16[2,6,16,16,128]{2,0,1,4,3:T(2,128)(2,1)} %bitcast.42) | data formatting | bytes 1572864 | tf_op jit(solution)/shard_map/all_to_all | solution.py:18
  87.9 0.0 reduce-scatter.4.cloned.1.call-start
  88.0 22.4 %all_gather.7 = bf16[2,3,256,128]{3,2,1,0:T(8,128)(2,1)S(1)} all-gather(bf16[2,3,16,128]{3,2,1,0:T(8,128)(2,1)S(1)} %broadcast_multiply_fusion), channel_id=1, replica_groups=mesh['ev'=16,'st'=2] {'ev'}, dimensions={2}, use_global_device_ids=true | all-gather | bytes 417792 | tf_op jit(solution)/shard_map/all_gather | solution.py:22
  110.4 1.8 %convolution_bitcast_fusion = f32[2,2,256,1536]{3,2,1,0:T(8,128)S(1)} fusion(bf16[2,3,128,1536,1]{2,3,1,0,4:T(8,128)(2,1)S(1)} %bitcast.48, bf16[2,3,256,128]{3,2,1,0:T(8,128)(2,1)S(1)} %all_gather.7), kind=kOutput, calls=%fused_computation | convolution fusion | flops 1207959552 | bytes 9043968 | tf_op jit(solution)/shard_map/rfps,qfsn->rqpn/dot_general | solution.py:24
  112.2 1.7 %slice_subtract_fusion = (f32[1,1,256,1536]{3,2,1,0:T(8,128)}, f32[1,1,256,1536]{3,2,1,0:T(8,128)S(1)}) fusion(f32[2,2,256,1536]{3,2,1,0:T(8,128)S(1)} %convolution_bitcast_fusion), kind=kLoop, calls=%fused_computation.3 | loop fusion | flops 786432 | bytes 9437184 | tf_op jit(solution)/shard_map/sub | solution.py:27
  113.9 1.9 %copy.35 = f32[1,1,256,1536]{2,3,1,0:T(8,128)S(1)} copy(f32[1,1,256,1536]{3,2,1,0:T(8,128)} %get-tuple-element.5) | data formatting | bytes 3145728 | tf_op jit(solution)/shard_map/sub | solution.py:27
  115.8 1.6 %copy.39 = f32[256,6,256]{2,0,1:T(8,128)} copy(f32[256,6,256]{0,2,1:T(8,128)S(1)} %bitcast.44) | data formatting | bytes 3145728 | tf_op jit(solution)/shard_map/sub | solution.py:27
  117.4 0.8 slice_reduce_fusion.2
  118.2 1.1 copy.36
  119.3 0.5 copy.37
  119.8 0.5 copy.40
  120.2 0.8 slice_reduce_fusion
  121.0 1.1 copy.38
  122.1 0.0 all-gather.2.cloned.1.call-done
  122.1 1.7 %convert_element_type.6 = f32[2,6,256,256]{3,2,1,0:T(8,128)S(1)} convert(bf16[2,6,256,256]{3,2,1,0:T(8,128)(2,1)} %all-gather.2.cloned.1.call-done) | non-fusion elementwise | flops 786432 | bytes 4718592 | tf_op jit(solution)/shard_map/convert_element_type | solution.py:29
  123.8 0.2 slice_bitcast_fusion.1
  124.1 0.1 slice_reduce_fusion.1
  124.2 1.3 copy-done
  125.5 0.7 multiply_reduce_fusion
  126.1 0.1 subtract_reduce_fusion
  126.2 0.8 copy.48
  127.0 7.8 %reduce-scatter.4.cloned.1.call-done = f32[128,2]{1,0:T(8,128)} async-done(((f32[256,2]{1,0:T(8,128)}), f32[128,2]{1,0:T(8,128)}) %reduce-scatter.4.cloned.1.call-update) | async-done | bytes 1040
  134.8 1.5 %copy.49 = f32[2,128]{1,0:T(2,128)} copy(f32[2,128]{0,1:T(8,128)} %bitcast.51) | data formatting | bytes 2048
  (12 shorter events, 0.1 us)
Async XLA Ops:
  41.2 7.6 %copy-start.2 = (s32[16,128]{1,0:T(8,128)S(1)}, s32[16,128]{1,0:T(8,128)}, u32[]{:S(2)}) copy-start(s32[16,128]{1,0:T(8,128)} %param.8) | copy-start | bytes 24580
  41.2 26.2 %all-to-all-start = ((bf16[16,2,12288]{2,1,0:T(2,128)(2,1)}), bf16[16,2,12288]{2,1,0:T(2,128)(2,1)S(1)}, u32[]{:S(2)}, u32[]{:S(2)}) async-start(bf16[16,2,12288]{2,1,0:T(2,128)(2,1)} %reshape.28), calls=%async_computation | async-start | bytes 1572864 | tf_op jit(solution)/shard_map/all_to_all | solution.py:18
  48.7 73.4 %all-gather.2.cloned.1.call-start = ((), (), s32[]{:S(2)}) async-start(), calls=%async_computation.2 | async-start | bytes 2359296 | tf_op jit(solution)/shard_map/all_gather | solution.py:19
  73.0 14.9 %copy-start.1 = (bf16[2,3,16,128]{3,2,1,0:T(8,128)(2,1)S(1)}, bf16[2,3,16,128]{3,2,1,0:T(8,128)(2,1)}, u32[]{:S(2)}) copy-start(bf16[2,3,16,128]{3,2,1,0:T(8,128)(2,1)} %param.7) | copy-start | bytes 73732
  87.9 46.9 %reduce-scatter.4.cloned.1.call-start = ((), (), s32[]{:S(2)}) async-start(), calls=%async_computation.3 | async-start | bytes 196608
  124.1 1.4 copy-start
  124.1 1.4 copy-start.3
Sparse Core Ops, SparseCore 0:
  88.0 27.8 all-gather.1
  127.1 7.6 reduce-scatter.3
where the time goes:
time: 144 us; the launch traced here: 143 us
  local copies, waits for them, and re-layouts  68.5 us (48%)
  waiting for transfers between devices  23.4 us (16%)
  blocking collectives  22.4 us (16%)
  between operations  13.6 us (9%)
  starting transfers between devices  7.63 us (5%)
  other arithmetic  5.83 us (4%)
  matrix products  1.83 us (1%)
    unnamed x13, local copies, waits for them, and re-layouts  30.6 us
    all_gather x1, blocking collectives, local(): weight_rows = lax.all_gather(masked, 'ev', axis=2, tiled=True)  22.4 us
    all_to_all x1, waiting for transfers between devices, local(): lax.all_to_all(selected, 'ev', split_axis=3, concat_axis=2, tiled=True)  15.5 us
    all_to_all x1, local copies, waits for them, and re-layouts, local(): lax.all_to_all(selected, 'ev', split_axis=3, concat_axis=2, tiled=True)  14.8 us
    reshape x1, local copies, waits for them, and re-layouts, local(): selected = selected.reshape(2, 6, event_rows, ev_count * sub_cells)  11.5 us
    unnamed x3, waiting for transfers between devices  7.81 us
    all_to_all x1, starting transfers between devices, local(): lax.all_to_all(selected, 'ev', split_axis=3, concat_axis=2, tiled=True)  7.55 us
    sub x2, local copies, waits for them, and re-layouts, local(): products[0, 0] - products[1, 1]  3.5 us
  transfers between devices with their start and end apart: 3, of which 2 were waited for; matrix products, arithmetic and copies ran while one was open for 10% of the time, Pallas kernels for 0%

commit v1 on v0

--- a/solution.py
+++ b/solution.py
@@ -5,6 +5,16 @@
 
 
 def local(strain, green, weights, mask):
+
+    def face_form(piece_in):
+        m_next = jnp.concatenate(
+            lax.all_to_all(
+                jnp.stack(jnp.split(piece_in, lax.psum(1, "ev"), 3), axis=0), "ev", 0, 0
+            ),
+            2,
+        )
+        return m_next
+
     masked = weights * mask.astype(jnp.bfloat16)[None, None]
     cells_dev = green.shape[4]
     station_count = green.shape[2]
@@ -15,7 +25,7 @@
     shaped = strain.reshape(2, 6, event_rows, ev_count, st_count, sub_cells)
     selected = lax.dynamic_index_in_dim(shaped, lax.axis_index("st"), 4, keepdims=False)
     selected = selected.reshape(2, 6, event_rows, ev_count * sub_cells)
-    narrow = lax.all_to_all(selected, "ev", split_axis=3, concat_axis=2, tiled=True)
+    narrow = face_form(selected)
     strain_all = lax.all_gather(narrow, "st", axis=3, tiled=True)
     green_flat = green.reshape(2, 3, station_count, 6 * cells_dev)
     voigt = jnp.array([1.0, 1.0, 1.0, 2.0, 2.0, 2.0], jnp.float32)

time: 144 us -> 105 us (0.73)
  local copies, waits for them, and re-layouts: 68.5 us -> 31.9 us
    all_to_all x1 -> x0, local copies, waits for them, and re-layouts: 14.8 us -> none  [local(): lax.all_to_all(selected, 'ev', split_axis=3, concat_axis=2, tiled=True)]
    unnamed x13 -> x28, local copies, waits for them, and re-layouts: 30.6 us -> 16.3 us
    reshape x1, local copies, waits for them, and re-layouts: 11.5 us -> 0.33 us  [local(): selected = selected.reshape(2, 6, event_rows, ev_count * sub_cells)]
    dynamic_slice x1, local copies, waits for them, and re-layouts: 1.89 us -> 4.71 us  [local(): lax.dynamic_index_in_dim(shaped, lax.axis_index('st'), 4, keepdims=False)]
  transfers between devices with their start and end apart: 3 -> 3, of which waited for: 2 -> 2; matrix products, arithmetic and copies ran while one was open for 10% -> 12% of each run, Pallas kernels for 0% -> 0%
where the time goes in v1:
time: 105 us
  local copies, waits for them, and re-layouts  31.9 us (30%)
  waiting for transfers between devices  23.3 us (22%)
  blocking collectives  22.4 us (21%)
  between operations  13.6 us (13%)
  starting transfers between devices  7.5 us (7%)
  other arithmetic  4.4 us (4%)
  matrix products  1.83 us (2%)
    all_gather x1, blocking collectives, local(): weight_rows = lax.all_gather(masked, 'ev', axis=2, tiled=True)  22.4 us
    unnamed x28, local copies, waits for them, and re-layouts  16.3 us
    all_to_all x1, waiting for transfers between devices, face_form(): lax.all_to_all(jnp.stack(jnp.split(piece_in, lax.psum(1, 'ev'), 3), axis=...  15.5 us
    unnamed x3, waiting for transfers between devices  7.81 us
    all_to_all x1, starting transfers between devices, face_form(): lax.all_to_all(jnp.stack(jnp.split(piece_in, lax.psum(1, 'ev'), 3), axis=...  7.41 us
    dynamic_slice x1, local copies, waits for them, and re-layouts, local(): lax.dynamic_index_in_dim(shaped, lax.axis_index('st'), 4, keepdims=False)  4.71 us
    sub x2, local copies, waits for them, and re-layouts, local(): products[0, 0] - products[1, 1]  3.48 us
    reshape x1, local copies, waits for them, and re-layouts, local(): shaped = strain.reshape(2, 6, event_rows, ev_count, st_count, sub_cells)  2.82 us
  transfers between devices with their start and end apart: 3, of which 2 were waited for; matrix products, arithmetic and copies ran while one was open for 12% of the time, Pallas kernels for 0%

profile of v1, /device:TPU:0, one launch (start us, length us, event | category | flops | bytes accessed | tf_op | source)
XLA Modules:
  0.0 105.0 jit_solution(15221466284462118104)
XLA Ops:
  6.5 2.8 %reshape.26 = bf16[2,6,16,16,2,128]{5,4,3,2,1,0:T(2,128)(2,1)S(1)} reshape(bf16[2,6,16,4096]{3,2,1,0:T(8,128)(2,1)} %param.5) | data formatting | bytes 3145728 | tf_op jit(solution)/shard_map/reshape | solution.py:25
  9.4 4.7 %dynamic-slice_reduce_fusion = bf16[2,6,16,16,128]{4,3,2,1,0:T(8,128)(2,1)S(1)} fusion(bf16[2,6,16,16,2,128]{5,4,3,2,1,0:T(2,128)(2,1)S(1)} %reshape.26, s32[]{:T(128)S(6)} %select_n.4), kind=kLoop, calls=%fused_computation.6 | loop fusion | bytes 1572868 | tf_op jit(solution)/shard_map/jit(dynamic_index_in_dim)/dynamic_slice | solution.py:26
  14.4 0.6 fusion.16
  15.1 0.6 fusion.15
  15.7 0.6 fusion.14
  16.3 0.6 fusion.13
  16.9 0.6 fusion.12
  17.6 0.6 fusion.11
  18.2 0.6 fusion.10
  19.4 0.6 fusion.8
  20.1 0.6 fusion.7
  21.3 0.6 fusion.5
  22.0 0.6 fusion.4
  22.6 0.6 fusion.3
  23.2 0.6 fusion.2
  23.8 0.6 fusion.1
  24.5 7.4 %all-to-all-start = ((bf16[16,2,6,16,128]{4,3,2,1,0:T(8,128)(2,1)}), bf16[16,2,6,16,128]{4,3,2,1,0:T(8,128)(2,1)S(1)}, u32[]{:S(2)}, u32[]{:S(2)}) async-start(bf16[16,2,6,16,128]{4,3,2,1,0:T(8,128)(2,1)} %fusion.1), calls=%async_computation | async-start | bytes 1572864 | tf_op jit(solution)/shard_map/all_to_all | solution.py:11
  31.9 3.1 %copy.44 = bf16[2,3,128,6,256]{2,4,3,1,0:T(8,128)(2,1)S(1)} copy(bf16[2,3,128,6,256]{4,2,3,1,0:T(8,128)(2,1)} %param.6) | data formatting | bytes 4718592 | tf_op args[1]
  35.0 15.5 %all-to-all-done = bf16[16,2,6,16,128]{4,3,2,1,0:T(8,128)(2,1)S(1)} async-done(((bf16[16,2,6,16,128]{4,3,2,1,0:T(8,128)(2,1)}), bf16[16,2,6,16,128]{4,3,2,1,0:T(8,128)(2,1)S(1)}, u32[]{:S(2)}, u32[]{:S(2)}) %all-to-all-start) | async-done | bytes 786464 | tf_op jit(solution)/shard_map/all_to_all | solution.py:11
  50.6 1.1 %copy.43 = bf16[2,6,16,16,128]{4,3,2,1,0:T(8,128)(2,1)} copy(bf16[2,6,16,16,128]{4,3,1,0,2:T(8,128)(2,1)S(1)} %bitcast.108) | data formatting | bytes 1572864 | tf_op jit(solution)/shard_map/reshape | solution.py:10
  51.7 22.4 %all_gather.7 = bf16[2,3,256,128]{3,2,1,0:T(8,128)(2,1)S(1)} all-gather(bf16[2,3,16,128]{3,2,1,0:T(8,128)(2,1)S(1)} %broadcast_multiply_fusion), channel_id=1, replica_groups=mesh['ev'=16,'st'=2] {'ev'}, dimensions={2}, use_global_device_ids=true | all-gather | bytes 417792 | tf_op jit(solution)/shard_map/all_gather | solution.py:32
  74.2 1.8 %convolution_bitcast_fusion = f32[2,2,256,1536]{3,2,1,0:T(8,128)S(1)} fusion(bf16[2,3,128,1536,1]{2,3,1,0,4:T(8,128)(2,1)S(1)} %bitcast.106, bf16[2,3,256,128]{3,2,1,0:T(8,128)(2,1)S(1)} %all_gather.7), kind=kOutput, calls=%fused_computation | convolution fusion | flops 1207959552 | bytes 9043968 | tf_op jit(solution)/shard_map/rfps,qfsn->rqpn/dot_general | solution.py:34
  76.0 1.7 %slice_subtract_fusion = (f32[1,1,256,1536]{3,2,1,0:T(8,128)}, f32[1,1,256,1536]{3,2,1,0:T(8,128)S(1)}) fusion(f32[2,2,256,1536]{3,2,1,0:T(8,128)S(1)} %convolution_bitcast_fusion), kind=kLoop, calls=%fused_computation.3 | loop fusion | flops 786432 | bytes 9437184 | tf_op jit(solution)/shard_map/sub | solution.py:37
  78.2 1.6 %copy.51 = f32[256,6,256]{2,0,1:T(8,128)} copy(f32[256,6,256]{0,2,1:T(8,128)S(1)} %bitcast.102) | data formatting | bytes 3145728 | tf_op jit(solution)/shard_map/add | solution.py:38
  79.8 1.9 %copy.46 = f32[1,1,256,1536]{2,3,1,0:T(8,128)S(1)} copy(f32[1,1,256,1536]{3,2,1,0:T(8,128)} %get-tuple-element.5) | data formatting | bytes 3145728 | tf_op jit(solution)/shard_map/sub | solution.py:37
  81.7 1.6 %copy.50 = f32[256,6,256]{2,0,1:T(8,128)} copy(f32[256,6,256]{0,2,1:T(8,128)S(1)} %bitcast.104) | data formatting | bytes 3145728 | tf_op jit(solution)/shard_map/sub | solution.py:37
  83.7 1.7 %convert_element_type.6 = f32[2,6,256,256]{3,2,1,0:T(8,128)S(1)} convert(bf16[2,6,256,256]{3,2,1,0:T(8,128)(2,1)} %all-gather.2.cloned.1.call-done) | non-fusion elementwise | flops 786432 | bytes 4718592 | tf_op jit(solution)/shard_map/convert_element_type | solution.py:39
  85.8 1.1 %copy-done.1 = f32[256,6,256]{2,0,1:T(8,128)S(1)} copy-done((f32[256,6,256]{2,0,1:T(8,128)S(1)}, f32[256,6,256]{2,0,1:T(8,128)}, u32[]{:S(2)}) %copy-start.1) | copy-done | bytes 1572888
  87.4 0.7 multiply_reduce_fusion
  88.1 0.8 copy.56
  88.9 7.8 %reduce-scatter.4.cloned.1.call-done = f32[128,2]{1,0:T(8,128)} async-done(((f32[256,2]{1,0:T(8,128)}), f32[128,2]{1,0:T(8,128)}) %reduce-scatter.4.cloned.1.call-update) | async-done | bytes 1040
  96.7 1.5 %copy.57 = f32[2,128]{1,0:T(2,128)} copy(f32[2,128]{0,1:T(8,128)} %bitcast.110) | data formatting | bytes 2048
  (28 shorter events, 3.5 us)
Async XLA Ops:
  24.5 26.1 %all-to-all-start = ((bf16[16,2,6,16,128]{4,3,2,1,0:T(8,128)(2,1)}), bf16[16,2,6,16,128]{4,3,2,1,0:T(8,128)(2,1)S(1)}, u32[]{:S(2)}, u32[]{:S(2)}) async-start(bf16[16,2,6,16,128]{4,3,2,1,0:T(8,128)(2,1)} %fusion.1), calls=%async_computation | async-start | bytes 1572864 | tf_op jit(solution)/shard_map/all_to_all | solution.py:11
  31.9 3.1 %copy-start.3 = (s32[16,128]{1,0:T(8,128)S(1)}, s32[16,128]{1,0:T(8,128)}, u32[]{:S(2)}) copy-start(s32[16,128]{1,0:T(8,128)} %param.8) | copy-start | bytes 24580
  31.9 51.8 %all-gather.2.cloned.1.call-start = ((), (), s32[]{:S(2)}) async-start(), calls=%async_computation.2 | async-start | bytes 2359296 | tf_op jit(solution)/shard_map/all_gather | solution.py:29
  35.0 16.7 %copy-start.2 = (bf16[2,3,16,128]{3,2,1,0:T(8,128)(2,1)S(1)}, bf16[2,3,16,128]{3,2,1,0:T(8,128)(2,1)}, u32[]{:S(2)}) copy-start(bf16[2,3,16,128]{3,2,1,0:T(8,128)(2,1)} %param.7) | copy-start | bytes 73732
  51.7 45.1 %reduce-scatter.4.cloned.1.call-start = ((), (), s32[]{:S(2)}) async-start(), calls=%async_computation.3 | async-start | bytes 196608
  85.4 1.4 %copy-start.1 = (f32[256,6,256]{2,0,1:T(8,128)S(1)}, f32[256,6,256]{2,0,1:T(8,128)}, u32[]{:S(2)}) copy-start(f32[256,6,256]{2,0,1:T(8,128)} %copy.50) | copy-start | bytes 4718596
  85.7 1.7 %copy-start = (f32[256,6,256]{2,0,1:T(8,128)S(1)}, f32[256,6,256]{2,0,1:T(8,128)}, u32[]{:S(2)}) copy-start(f32[256,6,256]{2,0,1:T(8,128)} %copy.51) | copy-start | bytes 4718596
  85.7 1.7 %copy-start.4 = (f32[6]{0:T(128)S(1)}, f32[6]{0:T(128)}, u32[]{:S(2)}) copy-start(f32[6]{0:T(128)} %constant.14.clone) | copy-start | bytes 76
Sparse Core Ops, SparseCore 0:
  51.8 27.8 all-gather.1
  89.1 7.6 reduce-scatter.3
